TPU v7x, 32 devices: a whole 2x2x4 slice. The times are simulated.
32 devices in a mesh: lat: 8 (over z, x), lon: 4 (over y, core).
Axes of the slice: x: 2, y: 2, z: 4, core: 2. Of those that a mesh axis runs over, the one named last changes fastest.
Arguments:
- state: bfloat16 [32, 32, 64, 128], P('lat', 'lon'), may hold values from -6 to 6
- obs_row: int32 [32, 32, 128], P('lat', 'lon'), may hold values from 0 to 63
- obs_count: int32 [32, 32], P('lat', 'lon'), may hold values from 0 to 128
- obs_value: float32 [32, 32, 128], P('lat', 'lon'), may hold values from -6 to 6
- obs_weight: float32 [32, 32, 128], P('lat', 'lon'), may hold values from 0.5 to 2
- quadrant: int32 [32, 32, 64], P('lat', 'lon'), may hold values from 0 to 3
- frac_lat: float32 [32, 32, 64], P('lat', 'lon'), may hold values from 0 to 1
- frac_lon: float32 [32, 32, 64], P('lat', 'lon'), may hold values from 0 to 1
- land: int32 [32, 32, 64], P('lat', 'lon'), may hold values 0 or 1
Outputs:
- analysis: bfloat16 [32, 32, 64, 128], P('lat', 'lon')
All inputs are finite; a program needn't handle non-finite values. No bound on the sum of `land` on one device may be relied on, other than what follows from the above.
Results may differ from a plain program's by a relative error of at most 0.0051.
Values may be sent and summed in bfloat16 or wider, within the bound.
A program may use at most 64 MiB of HBM per device.

v0:
```python
import functools
import math

import jax
import jax.numpy as jnp
from jax import lax
from jax.experimental import pallas as pl
from jax.experimental.pallas import tpu as pltpu
from jax.sharding import PartitionSpec as P

ITERS = 6
NEAR = (0.5, 1.0, 0.5)
SIDE_ROWS = 16
F32 = jnp.float32
BF16 = jnp.bfloat16
MESH = pl.DeviceIdType.MESH
WAYS = ((-1, 0), (1, 0), (-1, -1), (-1, 1), (1, -1), (1, 1), (0, -1), (0, 1))


def nn(a, b):
    return lax.dot_general(a, b, (((1,), (0,)), ((), ())), preferred_element_type=F32)


def nt(a, b):
    return lax.dot_general(a, b, (((1,), (1,)), ((), ())), preferred_element_type=F32)


def tn(a, b):
    return lax.dot_general(a, b, (((0,), (0,)), ((), ())), preferred_element_type=F32)


def group_of(count, most=4):
    return next(g for g in range(most, 0, -1) if count % g == 0)


def prep_kernel(count_ref, state_ref, row_ref, value_ref, weight_ref, out_ref):
    tile_lat, tile_lon, cells, members = state_ref.shape
    slots = row_ref.shape[-1]
    nodes = tile_lat * tile_lon
    group = group_of(nodes)

    def step(t, carry):
        for g in range(group):
            node = t * group + g
            i, j = node // tile_lon, node % tile_lon
            values = state_ref[i, j].astype(F32)
            mean = jnp.sum(values, axis=1, keepdims=True) * (1.0 / members)
            pert = values - mean
            lane = lax.broadcasted_iota(jnp.int32, (1, slots), 1)
            weight = jnp.where(lane < count_ref[i, j], weight_ref[i, pl.ds(j, 1), :], 0.0)
            square = weight * weight
            hit = row_ref[i, pl.ds(j, 1), :] == lax.broadcasted_iota(jnp.int32, (cells, slots), 0)
            density = jnp.sum(jnp.where(hit, square, 0.0), axis=1, keepdims=True)
            pulled = jnp.sum(
                jnp.where(hit, square * value_ref[i, pl.ds(j, 1), :], 0.0), axis=1, keepdims=True
            )
            out_ref[i, j, pl.ds(0, cells), :] = (jnp.sqrt(density) * pert).astype(BF16)
            side = jnp.sum(pert * (pulled - density * mean), axis=0, keepdims=True)
            high = side.astype(BF16).astype(F32)
            which = lax.broadcasted_iota(jnp.int32, (SIDE_ROWS, members), 0)
            tail = jnp.where(which == 0, high, jnp.where(which == 1, side - high, 0.0))
            out_ref[i, j, pl.ds(cells, SIDE_ROWS), :] = tail.astype(BF16)
        return carry

    lax.fori_loop(0, nodes // group, step, 0)


def edge_slices(step, size):
    if step == 0:
        return slice(0, size), slice(1, size + 1), size
    if step < 0:
        return 0, size + 1, 1
    return size - 1, 0, 1


def main_kernel(
    counts, qx_ref, state_ref, quadrant_ref, frac_lat_ref, frac_lon_ref, land_ref,
    out_ref, qbuf, wbuf, q_send, q_recv, w_send, w_recv,
):
    n_lat, n_lon = counts
    tile_lat, tile_lon, cells, members = state_ref.shape
    lat, lon = lax.axis_index("lat"), lax.axis_index("lon")

    def exists(way):
        if way[0] < 0:
            return lat > 0
        if way[0] > 0:
            return lat < n_lat - 1
        return None

    def where_exists(way, do):
        if way[0] == 0:
            do()
        else:
            pl.when(exists(way))(do)

    def peer(way):
        return (lat + way[0], lax.rem(lon + way[1] + n_lon, n_lon))

    def at(ref, i, j):
        i = pl.ds(i.start, i.stop - i.start) if isinstance(i, slice) else i
        j = pl.ds(j.start, j.stop - j.start) if isinstance(j, slice) else j
        return ref.at[i, j]

    def copy(source, offset, buffer, send, recv, index):
        way = WAYS[index]
        si, di, _ = edge_slices(way[0], tile_lat)
        sj, dj, _ = edge_slices(way[1], tile_lon)

        def moved(s):
            return slice(s.start + offset, s.stop + offset) if isinstance(s, slice) else s + offset

        return pltpu.make_async_remote_copy(
            src_ref=at(source, moved(si), moved(sj)),
            dst_ref=at(buffer, di, dj),
            send_sem=send.at[index],
            recv_sem=recv.at[index],
            device_id=peer(way),
            device_id_type=MESH,
        )

    def q_copy(index):
        return copy(qx_ref, 0, qbuf, q_send, q_recv, index)

    def w_copy(index):
        return copy(wbuf, 1, wbuf, w_send, w_recv, index)

    barrier = pltpu.get_barrier_semaphore()
    for way in WAYS:
        where_exists(way, lambda way=way: pl.semaphore_signal(
            barrier, inc=1, device_id=peer(way), device_id_type=MESH))
    present = 2 + 3 * (lat > 0).astype(jnp.int32) + 3 * (lat < n_lat - 1).astype(jnp.int32)
    pl.semaphore_wait(barrier, present)
    for index, way in enumerate(WAYS):
        where_exists(way, lambda index=index: q_copy(index).start())

    @pl.when(lat == 0)
    def _():
        qbuf[0] = jnp.zeros(qbuf.shape[1:], BF16)
        wbuf[0] = jnp.zeros(wbuf.shape[1:], BF16)

    @pl.when(lat == n_lat - 1)
    def _():
        qbuf[tile_lat + 1] = jnp.zeros(qbuf.shape[1:], BF16)
        wbuf[tile_lat + 1] = jnp.zeros(wbuf.shape[1:], BF16)

    for i in range(tile_lat):
        qbuf[i + 1, pl.ds(1, tile_lon)] = qx_ref[i]

    def received(index, make):
        way = WAYS[index]
        back = (-way[0], -way[1])
        where_exists(back, lambda: make(index).wait_recv())

    def sent(index, make):
        where_exists(WAYS[index], lambda: make(index).wait_send())

    eye = (
        lax.broadcasted_iota(jnp.int32, (members, members), 0)
        == lax.broadcasted_iota(jnp.int32, (members, members), 1)
    ).astype(F32)

    def gram_of(i, j):
        left, right = [], []
        tail = jnp.zeros((SIDE_ROWS, members), F32)
        for b in range(3):
            for a in range(3):
                scale = NEAR[a] * NEAR[b]
                block = qbuf[i + a, j + b, pl.ds(0, cells), :]
                right.append(block)
                left.append(block if scale == 1.0 else block * jnp.asarray(scale, BF16))
                tail += scale * qbuf[i + a, j + b, pl.ds(cells, SIDE_ROWS), :].astype(F32)
        gram = tn(jnp.concatenate(left, axis=0), jnp.concatenate(right, axis=0))
        side = jnp.sum(tail, axis=0, keepdims=True)
        return gram + (members - 1.0) * eye, side

    def total(x):
        return jnp.sum(jnp.sum(x, axis=0, keepdims=True), axis=1, keepdims=True)

    def transform(places):
        grams, sides, frobs, spots = [], [], [], []
        for i, j in places:
            gram, side = gram_of(i, j)
            grams.append(gram)
            sides.append(side)
        cy, ey, cz, ez = [], [], [], []
        for gram in grams:
            frob = jnp.sqrt(total(gram * gram))
            frobs.append(frob)
            scaled = gram * (1.0 / frob)
            centre = total(scaled * eye) * (1.0 / members)
            rest = scaled - centre * eye
            cf, ef = 1.5 - 0.5 * centre, -0.5 * rest
            prod = nn(ef.astype(BF16), rest.astype(BF16))
            cy.append(cf * centre)
            ey.append(prod + cf * rest + centre * ef)
            cz.append(cf)
            ez.append(ef)
        for step in range(1, ITERS):
            last = step == ITERS - 1
            ybs = [e.astype(BF16) for e in ey]
            zbs = [e.astype(BF16) for e in ez]
            prods = [nn(zb, yb) for zb, yb in zip(zbs, ybs)]
            cfs = [1.5 - 0.5 * (y * z) for y, z in zip(cy, cz)]
            efs = [
                -0.5 * (prods[n] + cz[n] * ey[n] + cy[n] * ez[n]) for n in range(len(places))
            ]
            fbs = [e.astype(BF16) for e in efs]
            if last:
                both = [nn(fb, zb) for fb, zb in zip(fbs, zbs)]
            else:
                both = [
                    nn(fb, jnp.concatenate([zb, yb], axis=1))
                    for fb, zb, yb in zip(fbs, zbs, ybs)
                ]
            for n in range(len(places)):
                if not last:
                    ey[n] = both[n][:, members:] + cfs[n] * ey[n] + cy[n] * efs[n]
                    cy[n] = cfs[n] * cy[n]
                ez[n] = both[n][:, :members] + cfs[n] * ez[n] + cz[n] * efs[n]
                cz[n] = cfs[n] * cz[n]
        for n, (i, j) in enumerate(places):
            root = ez[n] + cz[n] * eye
            high = root.astype(BF16)
            low = (root - high.astype(F32)).astype(BF16)
            pair = jnp.concatenate([high, low], axis=1)
            side = jnp.broadcast_to(sides[n], (members, members))
            s_high = side.astype(BF16)
            s_low = (side - s_high.astype(F32)).astype(BF16)
            inner = nt(pair, jnp.concatenate([s_high, s_high], axis=1)) + nt(high, s_low)
            i_high = inner.astype(BF16)
            i_low = (inner - i_high.astype(F32)).astype(BF16)
            mean_weight = nn(pair, jnp.concatenate([i_high, i_high], axis=0)) + nn(high, i_low)
            inv = 1.0 / frobs[n]
            weights = mean_weight * inv + (math.sqrt(members - 1) * jnp.sqrt(inv)) * root
            wbuf[i + 1, j + 1] = weights.astype(BF16)

    mid_lat, mid_lon = tile_lat - 2, tile_lon - 2
    n_rows, n_sides, n_inner = 2 * tile_lon, 2 * mid_lat, mid_lat * mid_lon
    group = next(g for g in (4, 2) if n_rows % g == 0 and n_sides % g == 0 and n_inner % g == 0)
    ahead = n_inner // group // 3
    g_rows, g_sides, g_inner = n_rows // group, n_sides // group, n_inner // group

    def row_place(k):
        return (k % 2) * (tile_lat - 1), k // 2

    def side_place(k):
        return 1 + k // 2, (k % 2) * (tile_lon - 1)

    def inner_place(k):
        return 1 + k // mid_lon, 1 + k % mid_lon

    def place(slot, g):
        rows = slot - ahead
        sides = rows - g_rows
        after = slot - g_rows - g_sides
        is_inner = (slot < ahead) | (sides >= g_sides)
        inner = inner_place(jnp.where(slot < ahead, slot, jnp.maximum(after, 0)) * group + g)
        row = row_place(jnp.clip(rows, 0, g_rows - 1) * group + g)
        side = side_place(jnp.clip(sides, 0, g_sides - 1) * group + g)
        i = jnp.where(is_inner, inner[0], jnp.where(sides >= 0, side[0], row[0]))
        j = jnp.where(is_inner, inner[1], jnp.where(sides >= 0, side[1], row[1]))
        return i, j

    def node_step(slot, carry):
        @pl.when(slot == ahead)
        def _():
            for index in range(len(WAYS)):
                received(index, q_copy)

        transform([place(slot, g) for g in range(group)])

        @pl.when(slot == ahead + g_rows - 1)
        def _():
            for index in range(6):
                where_exists(WAYS[index], lambda index=index: w_copy(index).start())

        @pl.when(slot == ahead + g_rows + g_sides - 1)
        def _():
            for index in range(6, 8):
                w_copy(index).start()

        return carry

    lax.fori_loop(0, g_rows + g_sides + g_inner, node_step, 0)

    def analyse(i, j):
        values = state_ref[i, j].astype(F32)
        mean = jnp.sum(values, axis=1, keepdims=True) * (1.0 / members)
        pert = (values - mean).astype(BF16)
        corner = quadrant_ref[i, pl.ds(j, 1), :]
        along = []
        for half, frac in (
            (corner // 2, frac_lat_ref[i, pl.ds(j, 1), :]),
            (corner % 2, frac_lon_ref[i, pl.ds(j, 1), :]),
        ):
            for a in range(3):
                along.append(
                    jnp.where(half == a, 1.0 - frac, 0.0) + jnp.where(half + 1 == a, frac, 0.0)
                )
        along.append(land_ref[i, pl.ds(j, 1), :].astype(F32))
        along.append(jnp.zeros_like(along[0]))
        coef = jnp.transpose(jnp.concatenate(along, axis=0))
        acc = mean
        for a in range(3):
            wide = jnp.concatenate([wbuf[i + a, j + b] for b in range(3)], axis=1)
            prod = nn(pert, wide)
            row = sum(
                coef[:, 3 + b : 4 + b] * prod[:, b * members : (b + 1) * members] for b in range(3)
            )
            acc = acc + coef[:, a : a + 1] * row
        result = jnp.where(coef[:, 6:7] == 1.0, acc, values)
        out_ref[i, j] = result.astype(BF16)

    def inner_step(t, carry):
        for g in range(group):
            analyse(*inner_place(t * group + g))
        return carry

    lax.fori_loop(0, g_inner, inner_step, 0)
    for index in range(len(WAYS)):
        received(index, w_copy)

    def rim_step(t, carry):
        for g in range(group):
            k = t * group + g
            row, side = row_place(jnp.minimum(k, n_rows - 1)), side_place(jnp.maximum(k - n_rows, 0))
            analyse(jnp.where(k < n_rows, row[0], side[0]), jnp.where(k < n_rows, row[1], side[1]))
        return carry

    lax.fori_loop(0, g_rows + g_sides, rim_step, 0)
    for index in range(len(WAYS)):
        sent(index, q_copy)
        sent(index, w_copy)


VM = pl.BlockSpec(memory_space=pltpu.VMEM)


def body(counts, state, obs_row, obs_count, obs_value, obs_weight, quadrant, frac_lat, frac_lon, land):
    tile_lat, tile_lon, cells, members = state.shape
    rows = cells + SIDE_ROWS
    qx = pl.pallas_call(
        prep_kernel,
        out_shape=jax.ShapeDtypeStruct((tile_lat, tile_lon, rows, members), BF16),
        in_specs=[pl.BlockSpec(memory_space=pltpu.SMEM)] + [VM] * 4,
        out_specs=VM,
        name="prep",
    )(obs_count, state, obs_row, obs_value, obs_weight)
    return pl.pallas_call(
        functools.partial(main_kernel, counts),
        out_shape=jax.ShapeDtypeStruct(state.shape, BF16),
        in_specs=[VM] * 6,
        out_specs=VM,
        scratch_shapes=[
            pltpu.VMEM((tile_lat + 2, tile_lon + 2, rows, members), BF16),
            pltpu.VMEM((tile_lat + 2, tile_lon + 2, members, members), BF16),
            pltpu.SemaphoreType.DMA((8,)),
            pltpu.SemaphoreType.DMA((8,)),
            pltpu.SemaphoreType.DMA((8,)),
            pltpu.SemaphoreType.DMA((8,)),
        ],
        compiler_params=pltpu.CompilerParams(
            collective_id=0, has_side_effects=True, vmem_limit_bytes=48 * 1024 * 1024
        ),
        name="analyse",
    )(qx, state, quadrant, frac_lat, frac_lon, land)


def solution(mesh):
    counts = (mesh.shape["lat"], mesh.shape["lon"])
    return jax.shard_map(
        functools.partial(body, counts),
        mesh=mesh,
        in_specs=(
            P("lat", "lon", None, None),
            P("lat", "lon", None),
            P("lat", "lon"),
            P("lat", "lon", None),
            P("lat", "lon", None),
            P("lat", "lon", None),
            P("lat", "lon", None),
            P("lat", "lon", None),
            P("lat", "lon", None),
        ),
        out_specs=P("lat", "lon", None, None),
        check_vma=False,
    )
```

profile of v0, /device:TPU:17, one launch (start us, length us, event | category | flops | bytes accessed | tf_op | source)
XLA Modules:
  0.0 51.1 jit_solution(7520424490010538001)
XLA Ops:
  0.0 0.0 copy-start.1
  0.0 0.0 copy-start.5
  0.0 0.0 copy-start.4
  0.0 0.0 copy-start.3
  0.0 0.0 copy-start.2
  0.0 3.6 %prep.1.qx_ref = bf16[4,8,80,128]{3,2,1,0:T(8,128)(2,1)} custom-call(s32[4,8]{1,0:T(4,128)} %count_ref.1, bf16[4,8,64,128]{3,2,1,0:T(8,128)(2,1)} %state_ref.3, s32[4,8,128]{2,1,0:T(8,128)} %row_ref.1, f32[4,8,128]{2,1,0:T(8,128)} %value_ref.1, f32[4,8,128]{2,1,0:T(8,128)} %weight_ref.1), custom_call_target="tpu_custom_call" | custom-call | tf_op jit(solution)/shard_map/prep/pallas_call | solution.py:343
  3.6 0.0 copy-done.1
  3.6 0.0 copy-done.5
  3.6 0.0 copy-done.4
  3.6 0.0 copy-done.3
  3.6 0.0 copy-done.2
  3.6 0.0 copy-start
  3.6 1.1 %copy-done = bf16[4,8,80,128]{3,2,1,0:T(8,128)(2,1)S(1)} copy-done((bf16[4,8,80,128]{3,2,1,0:T(8,128)(2,1)S(1)}, bf16[4,8,80,128]{3,2,1,0:T(8,128)(2,1)}, u32[]{:S(2)}) %copy-start) | copy-done | bytes 655384
  4.7 45.6 %analyse.1 = bf16[4,8,64,128]{3,2,1,0:T(8,128)(2,1)S(1)} custom-call(bf16[4,8,80,128]{3,2,1,0:T(8,128)(2,1)S(1)} %copy-done, bf16[4,8,64,128]{3,2,1,0:T(8,128)(2,1)S(1)} %copy-done.1, s32[4,8,64]{2,1,0:T(8,128)S(1)} %copy-done.2, f32[4,8,64]{2,1,0:T(8,128)S(1)} %copy-done.3, f32[4,8,64]{2,1,0:T(8,128)S(1)} %copy-done.4, s32[4,8,64]{2,1,0:T(8,128)S(1)} %copy-done.5), custom_call_target="tpu_custom_call" | custom-call | tf_op jit(solution)/shard_map/analyse/pallas_call | solution.py:350
  50.3 0.8 %copy.11 = bf16[4,8,64,128]{3,2,1,0:T(8,128)(2,1)} copy(bf16[4,8,64,128]{3,2,1,0:T(8,128)(2,1)S(1)} %analyse.1) | data formatting | bytes 1048576
Async XLA Ops:
  0.0 3.6 %copy-start.1 = (bf16[4,8,64,128]{3,2,1,0:T(8,128)(2,1)S(1)}, bf16[4,8,64,128]{3,2,1,0:T(8,128)(2,1)}, u32[]{:S(2)}) copy-start(bf16[4,8,64,128]{3,2,1,0:T(8,128)(2,1)} %state_ref.3) | copy-start | bytes 1572868
  0.0 3.6 %copy-start.5 = (s32[4,8,64]{2,1,0:T(8,128)S(1)}, s32[4,8,64]{2,1,0:T(8,128)}, u32[]{:S(2)}) copy-start(s32[4,8,64]{2,1,0:T(8,128)} %land_ref.1) | copy-start | bytes 24580
  0.0 3.6 %copy-start.4 = (f32[4,8,64]{2,1,0:T(8,128)S(1)}, f32[4,8,64]{2,1,0:T(8,128)}, u32[]{:S(2)}) copy-start(f32[4,8,64]{2,1,0:T(8,128)} %frac_lon_ref.1) | copy-start | bytes 24580
  0.0 3.6 %copy-start.3 = (f32[4,8,64]{2,1,0:T(8,128)S(1)}, f32[4,8,64]{2,1,0:T(8,128)}, u32[]{:S(2)}) copy-start(f32[4,8,64]{2,1,0:T(8,128)} %frac_lat_ref.1) | copy-start | bytes 24580
  0.0 3.6 %copy-start.2 = (s32[4,8,64]{2,1,0:T(8,128)S(1)}, s32[4,8,64]{2,1,0:T(8,128)}, u32[]{:S(2)}) copy-start(s32[4,8,64]{2,1,0:T(8,128)} %quadrant_ref.1) | copy-start | bytes 24580
  3.6 1.1 %copy-start = (bf16[4,8,80,128]{3,2,1,0:T(8,128)(2,1)S(1)}, bf16[4,8,80,128]{3,2,1,0:T(8,128)(2,1)}, u32[]{:S(2)}) copy-start(bf16[4,8,80,128]{3,2,1,0:T(8,128)(2,1)} %prep.1.qx_ref) | copy-start | bytes 1966084
where the time goes:
time: 51.5 us; the launch traced here: 51.1 us
  Pallas kernels  49.1 us (95%)
  local copies, waits for them, and re-layouts  1.9 us (4%)
    pallas_call x1, Pallas kernels, body(): pl.pallas_call(functools.partial(main_kernel, counts), out_shape=jax.Shap...  45.6 us
    pallas_call x1, Pallas kernels, body(): pl.pallas_call(prep_kernel, out_shape=jax.ShapeDtypeStruct((tile_lat, til...  3.57 us
    unnamed x13, local copies, waits for them, and re-layouts  1.9 us

commit v1 on v0

--- a/solution.py
+++ b/solution.py
@@ -75,9 +75,10 @@
 
 def main_kernel(
     counts, qx_ref, state_ref, quadrant_ref, frac_lat_ref, frac_lon_ref, land_ref,
-    out_ref, qbuf, wbuf, q_send, q_recv, w_send, w_recv,
+    out_ref, qbuf, wbuf, q_send, q_recv, w_send, w_recv, r_send, r_recv,
 ):
     n_lat, n_lon = counts
+    row_parts = r_send.shape[1]
     tile_lat, tile_lon, cells, members = state_ref.shape
     lat, lon = lax.axis_index("lat"), lax.axis_index("lon")
 
@@ -125,6 +126,19 @@
     def w_copy(index):
         return copy(wbuf, 1, wbuf, w_send, w_recv, index)
 
+    def row_copy(index, part):
+        source, target, _ = edge_slices(WAYS[index][0], tile_lat)
+        width = tile_lon // row_parts
+        columns = pl.ds(1 + part * width, width)
+        return pltpu.make_async_remote_copy(
+            src_ref=wbuf.at[source + 1, columns],
+            dst_ref=wbuf.at[target, columns],
+            send_sem=r_send.at[index, part],
+            recv_sem=r_recv.at[index, part],
+            device_id=peer(WAYS[index]),
+            device_id_type=MESH,
+        )
+
     barrier = pltpu.get_barrier_semaphore()
     for way in WAYS:
         where_exists(way, lambda way=way: pl.semaphore_signal(
@@ -159,6 +173,7 @@
         lax.broadcasted_iota(jnp.int32, (members, members), 0)
         == lax.broadcasted_iota(jnp.int32, (members, members), 1)
     ).astype(F32)
+    eye_b = eye.astype(BF16)
 
     def gram_of(i, j):
         left, right = [], []
@@ -171,29 +186,28 @@
                 left.append(block if scale == 1.0 else block * jnp.asarray(scale, BF16))
                 tail += scale * qbuf[i + a, j + b, pl.ds(cells, SIDE_ROWS), :].astype(F32)
         gram = tn(jnp.concatenate(left, axis=0), jnp.concatenate(right, axis=0))
-        side = jnp.sum(tail, axis=0, keepdims=True)
-        return gram + (members - 1.0) * eye, side
+        return gram, jnp.sum(tail, axis=0, keepdims=True)
 
     def total(x):
         return jnp.sum(jnp.sum(x, axis=0, keepdims=True), axis=1, keepdims=True)
 
     def transform(places):
-        grams, sides, frobs, spots = [], [], [], []
-        for i, j in places:
-            gram, side = gram_of(i, j)
-            grams.append(gram)
-            sides.append(side)
-        cy, ey, cz, ez = [], [], [], []
-        for gram in grams:
-            frob = jnp.sqrt(total(gram * gram))
+        group = range(len(places))
+        terms = [gram_of(i, j) for i, j in places]
+        frobs, cy, ey, cz, ez = [], [], [], [], []
+        for gram, _ in terms:
+            ridge = members - 1.0
+            trace = total(gram * eye)
+            frob = jnp.sqrt(total(gram * gram) + 2.0 * ridge * trace + ridge * ridge * members)
+            centre = ridge + trace * (1.0 / members)
+            inv = 1.0 / centre
+            rest = gram * inv + eye * (ridge * inv - 1.0)
             frobs.append(frob)
-            scaled = gram * (1.0 / frob)
-            centre = total(scaled * eye) * (1.0 / members)
-            rest = scaled - centre * eye
-            cf, ef = 1.5 - 0.5 * centre, -0.5 * rest
-            prod = nn(ef.astype(BF16), rest.astype(BF16))
-            cy.append(cf * centre)
-            ey.append(prod + cf * rest + centre * ef)
+            start = centre / frob
+            cf = 1.5 - 0.5 * start
+            ef = rest * (-0.5 * start / cf)
+            cy.append(cf * start)
+            ey.append((ef + rest) + nn(ef.astype(BF16), rest.astype(BF16)))
             cz.append(cf)
             ez.append(ef)
         for step in range(1, ITERS):
@@ -201,9 +215,10 @@
             ybs = [e.astype(BF16) for e in ey]
             zbs = [e.astype(BF16) for e in ez]
             prods = [nn(zb, yb) for zb, yb in zip(zbs, ybs)]
-            cfs = [1.5 - 0.5 * (y * z) for y, z in zip(cy, cz)]
+            cts = [y * z for y, z in zip(cy, cz)]
+            cfs = [1.5 - 0.5 * ct for ct in cts]
             efs = [
-                -0.5 * (prods[n] + cz[n] * ey[n] + cy[n] * ez[n]) for n in range(len(places))
+                ((ey[n] + ez[n]) + prods[n]) * (-0.5 * cts[n] / cfs[n]) for n in group
             ]
             fbs = [e.astype(BF16) for e in efs]
             if last:
@@ -213,31 +228,34 @@
                     nn(fb, jnp.concatenate([zb, yb], axis=1))
                     for fb, zb, yb in zip(fbs, zbs, ybs)
                 ]
-            for n in range(len(places)):
+            for n in group:
                 if not last:
-                    ey[n] = both[n][:, members:] + cfs[n] * ey[n] + cy[n] * efs[n]
+                    ey[n] = (efs[n] + ey[n]) + both[n][:, members:]
                     cy[n] = cfs[n] * cy[n]
-                ez[n] = both[n][:, :members] + cfs[n] * ez[n] + cz[n] * efs[n]
+                ez[n] = (efs[n] + ez[n]) + both[n][:, :members]
                 cz[n] = cfs[n] * cz[n]
+        which = lax.broadcasted_iota(jnp.int32, (SIDE_ROWS, members), 0)
         for n, (i, j) in enumerate(places):
-            root = ez[n] + cz[n] * eye
-            high = root.astype(BF16)
-            low = (root - high.astype(F32)).astype(BF16)
-            pair = jnp.concatenate([high, low], axis=1)
-            side = jnp.broadcast_to(sides[n], (members, members))
-            s_high = side.astype(BF16)
-            s_low = (side - s_high.astype(F32)).astype(BF16)
-            inner = nt(pair, jnp.concatenate([s_high, s_high], axis=1)) + nt(high, s_low)
-            i_high = inner.astype(BF16)
-            i_low = (inner - i_high.astype(F32)).astype(BF16)
-            mean_weight = nn(pair, jnp.concatenate([i_high, i_high], axis=0)) + nn(high, i_low)
-            inv = 1.0 / frobs[n]
-            weights = mean_weight * inv + (math.sqrt(members - 1) * jnp.sqrt(inv)) * root
-            wbuf[i + 1, j + 1] = weights.astype(BF16)
+            side = terms[n][1]
+            zb = ez[n].astype(BF16)
+            high = side.astype(BF16).astype(F32)
+            rows = jnp.where(which == 0, high, jnp.where(which == 1, side - high, 0.0))
+            inner = side + jnp.sum(nn(rows.astype(BF16), zb), axis=0, keepdims=True)
+            inner = inner * (cz[n] * cz[n] / frobs[n])
+            high = inner.astype(BF16)
+            low = (inner - high.astype(F32)).astype(BF16)
+            high = jnp.broadcast_to(high, (members, members))
+            low = jnp.broadcast_to(low, (members, members))
+            mean_weight = nt(
+                jnp.concatenate([zb, eye_b, eye_b], axis=1),
+                jnp.concatenate([high, high, low], axis=1),
+            )
+            spread = math.sqrt(members - 1) * cz[n] / jnp.sqrt(frobs[n])
+            wbuf[i + 1, j + 1] = (mean_weight + spread * (ez[n] + eye)).astype(BF16)
 
     mid_lat, mid_lon = tile_lat - 2, tile_lon - 2
     n_rows, n_sides, n_inner = 2 * tile_lon, 2 * mid_lat, mid_lat * mid_lon
-    group = next(g for g in (4, 2) if n_rows % g == 0 and n_sides % g == 0 and n_inner % g == 0)
+    group = n_rows // row_parts
     ahead = n_inner // group // 3
     g_rows, g_sides, g_inner = n_rows // group, n_sides // group, n_inner // group
 
@@ -270,9 +288,14 @@
 
         transform([place(slot, g) for g in range(group)])
 
+        for index in range(2):
+            part = slot - ahead
+            pl.when(exists(WAYS[index]) & (part >= 0) & (part < g_rows))(
+                lambda index=index, part=part: row_copy(index, part).start())
+
         @pl.when(slot == ahead + g_rows - 1)
         def _():
-            for index in range(6):
+            for index in range(2, 6):
                 where_exists(WAYS[index], lambda index=index: w_copy(index).start())
 
         @pl.when(slot == ahead + g_rows + g_sides - 1)
@@ -318,7 +341,10 @@
         return carry
 
     lax.fori_loop(0, g_inner, inner_step, 0)
-    for index in range(len(WAYS)):
+    for index in range(2):
+        for part in range(row_parts):
+            received(index, lambda index, part=part: row_copy(index, part))
+    for index in range(2, len(WAYS)):
         received(index, w_copy)
 
     def rim_step(t, carry):
@@ -331,7 +357,11 @@
     lax.fori_loop(0, g_rows + g_sides, rim_step, 0)
     for index in range(len(WAYS)):
         sent(index, q_copy)
-        sent(index, w_copy)
+        if index >= 2:
+            sent(index, w_copy)
+        else:
+            for part in range(row_parts):
+                sent(index, lambda index, part=part: row_copy(index, part))
 
 
 VM = pl.BlockSpec(memory_space=pltpu.VMEM)
@@ -340,6 +370,8 @@
 def body(counts, state, obs_row, obs_count, obs_value, obs_weight, quadrant, frac_lat, frac_lon, land):
     tile_lat, tile_lon, cells, members = state.shape
     rows = cells + SIDE_ROWS
+    sizes = (2 * tile_lon, 2 * (tile_lat - 2), (tile_lat - 2) * (tile_lon - 2))
+    row_parts = 2 * tile_lon // next(g for g in (4, 2) if all(n % g == 0 for n in sizes))
     qx = pl.pallas_call(
         prep_kernel,
         out_shape=jax.ShapeDtypeStruct((tile_lat, tile_lon, rows, members), BF16),
@@ -359,6 +391,8 @@
             pltpu.SemaphoreType.DMA((8,)),
             pltpu.SemaphoreType.DMA((8,)),
             pltpu.SemaphoreType.DMA((8,)),
+            pltpu.SemaphoreType.DMA((2, row_parts)),
+            pltpu.SemaphoreType.DMA((2, row_parts)),
         ],
         compiler_params=pltpu.CompilerParams(
             collective_id=0, has_side_effects=True, vmem_limit_bytes=48 * 1024 * 1024

time: 51.5 us -> 46.1 us (0.90)
  Pallas kernels: 49.1 us -> 44 us
    pallas_call x1, Pallas kernels: 45.6 us -> 40.4 us  [body(): pl.pallas_call(functools.partial(main_kernel, counts), out_shape=jax.Shap...]
where the time goes in v1:
time: 46.1 us; the launch traced here: 45.9 us
  Pallas kernels  44 us (95%)
  local copies, waits for them, and re-layouts  1.9 us (4%)
    pallas_call x1, Pallas kernels, body(): pl.pallas_call(functools.partial(main_kernel, counts), out_shape=jax.Shap...  40.4 us
    pallas_call x1, Pallas kernels, body(): pl.pallas_call(prep_kernel, out_shape=jax.ShapeDtypeStruct((tile_lat, til...  3.57 us
    unnamed x13, local copies, waits for them, and re-layouts  1.9 us

profile of v1, /device:TPU:17, one launch (start us, length us, event | category | flops | bytes accessed | tf_op | source)
XLA Modules:
  0.0 45.9 jit_solution(3362812940742890671)
XLA Ops:
  0.0 0.0 copy-start.1
  0.0 0.0 copy-start.5
  0.0 0.0 copy-start.4
  0.0 0.0 copy-start.3
  0.0 0.0 copy-start.2
  0.0 3.6 %prep.1.qx_ref = bf16[4,8,80,128]{3,2,1,0:T(8,128)(2,1)} custom-call(s32[4,8]{1,0:T(4,128)} %count_ref.1, bf16[4,8,64,128]{3,2,1,0:T(8,128)(2,1)} %state_ref.3, s32[4,8,128]{2,1,0:T(8,128)} %row_ref.1, f32[4,8,128]{2,1,0:T(8,128)} %value_ref.1, f32[4,8,128]{2,1,0:T(8,128)} %weight_ref.1), custom_call_target="tpu_custom_call" | custom-call | tf_op jit(solution)/shard_map/prep/pallas_call | solution.py:375
  3.6 0.0 copy-done.1
  3.6 0.0 copy-done.5
  3.6 0.0 copy-done.4
  3.6 0.0 copy-done.3
  3.6 0.0 copy-done.2
  3.6 0.0 copy-start
  3.6 1.1 %copy-done = bf16[4,8,80,128]{3,2,1,0:T(8,128)(2,1)S(1)} copy-done((bf16[4,8,80,128]{3,2,1,0:T(8,128)(2,1)S(1)}, bf16[4,8,80,128]{3,2,1,0:T(8,128)(2,1)}, u32[]{:S(2)}) %copy-start) | copy-done | bytes 655384
  4.7 40.4 %analyse.1 = bf16[4,8,64,128]{3,2,1,0:T(8,128)(2,1)S(1)} custom-call(bf16[4,8,80,128]{3,2,1,0:T(8,128)(2,1)S(1)} %copy-done, bf16[4,8,64,128]{3,2,1,0:T(8,128)(2,1)S(1)} %copy-done.1, s32[4,8,64]{2,1,0:T(8,128)S(1)} %copy-done.2, f32[4,8,64]{2,1,0:T(8,128)S(1)} %copy-done.3, f32[4,8,64]{2,1,0:T(8,128)S(1)} %copy-done.4, s32[4,8,64]{2,1,0:T(8,128)S(1)} %copy-done.5), custom_call_target="tpu_custom_call" | custom-call | tf_op jit(solution)/shard_map/analyse/pallas_call | solution.py:382
  45.1 0.8 %copy.11 = bf16[4,8,64,128]{3,2,1,0:T(8,128)(2,1)} copy(bf16[4,8,64,128]{3,2,1,0:T(8,128)(2,1)S(1)} %analyse.1) | data formatting | bytes 1048576
Async XLA Ops:
  0.0 3.6 %copy-start.1 = (bf16[4,8,64,128]{3,2,1,0:T(8,128)(2,1)S(1)}, bf16[4,8,64,128]{3,2,1,0:T(8,128)(2,1)}, u32[]{:S(2)}) copy-start(bf16[4,8,64,128]{3,2,1,0:T(8,128)(2,1)} %state_ref.3) | copy-start | bytes 1572868
  0.0 3.6 %copy-start.5 = (s32[4,8,64]{2,1,0:T(8,128)S(1)}, s32[4,8,64]{2,1,0:T(8,128)}, u32[]{:S(2)}) copy-start(s32[4,8,64]{2,1,0:T(8,128)} %land_ref.1) | copy-start | bytes 24580
  0.0 3.6 %copy-start.4 = (f32[4,8,64]{2,1,0:T(8,128)S(1)}, f32[4,8,64]{2,1,0:T(8,128)}, u32[]{:S(2)}) copy-start(f32[4,8,64]{2,1,0:T(8,128)} %frac_lon_ref.1) | copy-start | bytes 24580
  0.0 3.6 %copy-start.3 = (f32[4,8,64]{2,1,0:T(8,128)S(1)}, f32[4,8,64]{2,1,0:T(8,128)}, u32[]{:S(2)}) copy-start(f32[4,8,64]{2,1,0:T(8,128)} %frac_lat_ref.1) | copy-start | bytes 24580
  0.0 3.6 %copy-start.2 = (s32[4,8,64]{2,1,0:T(8,128)S(1)}, s32[4,8,64]{2,1,0:T(8,128)}, u32[]{:S(2)}) copy-start(s32[4,8,64]{2,1,0:T(8,128)} %quadrant_ref.1) | copy-start | bytes 24580
  3.6 1.1 %copy-start = (bf16[4,8,80,128]{3,2,1,0:T(8,128)(2,1)S(1)}, bf16[4,8,80,128]{3,2,1,0:T(8,128)(2,1)}, u32[]{:S(2)}) copy-start(bf16[4,8,80,128]{3,2,1,0:T(8,128)(2,1)} %prep.1.qx_ref) | copy-start | bytes 1966084

commit v2 on v1

--- a/solution.py
+++ b/solution.py
@@ -14,7 +14,8 @@
 F32 = jnp.float32
 BF16 = jnp.bfloat16
 MESH = pl.DeviceIdType.MESH
-WAYS = ((-1, 0), (1, 0), (-1, -1), (-1, 1), (1, -1), (1, 1), (0, -1), (0, 1))
+WAYS = ((-1, 0), (1, 0), (0, -1), (0, 1))
+CORNERS = ((-1, -1), (-1, 1), (1, -1), (1, 1))
 
 
 def nn(a, b):
@@ -76,6 +77,7 @@
 def main_kernel(
     counts, qx_ref, state_ref, quadrant_ref, frac_lat_ref, frac_lon_ref, land_ref,
     out_ref, qbuf, wbuf, q_send, q_recv, w_send, w_recv, r_send, r_recv,
+    c_send, c_recv,
 ):
     n_lat, n_lon = counts
     row_parts = r_send.shape[1]
@@ -139,11 +141,28 @@
             device_id_type=MESH,
         )
 
+    def corner_copy(buffer, stage, index):
+        side, step = CORNERS[index]
+        row = 0 if side < 0 else tile_lat + 1
+        source, target = (1, tile_lon + 1) if step < 0 else (tile_lon, 0)
+        return pltpu.make_async_remote_copy(
+            src_ref=buffer.at[row, source],
+            dst_ref=buffer.at[row, target],
+            send_sem=c_send.at[stage, index],
+            recv_sem=c_recv.at[stage, index],
+            device_id=peer((0, step)),
+            device_id_type=MESH,
+        )
+
+    def each_corner(buffer, stage, do):
+        for index, way in enumerate(CORNERS):
+            where_exists(way, lambda index=index: do(corner_copy(buffer, stage, index)))
+
     barrier = pltpu.get_barrier_semaphore()
     for way in WAYS:
         where_exists(way, lambda way=way: pl.semaphore_signal(
             barrier, inc=1, device_id=peer(way), device_id_type=MESH))
-    present = 2 + 3 * (lat > 0).astype(jnp.int32) + 3 * (lat < n_lat - 1).astype(jnp.int32)
+    present = 2 + (lat > 0).astype(jnp.int32) + (lat < n_lat - 1).astype(jnp.int32)
     pl.semaphore_wait(barrier, present)
     for index, way in enumerate(WAYS):
         where_exists(way, lambda index=index: q_copy(index).start())
@@ -256,7 +275,7 @@
     mid_lat, mid_lon = tile_lat - 2, tile_lon - 2
     n_rows, n_sides, n_inner = 2 * tile_lon, 2 * mid_lat, mid_lat * mid_lon
     group = n_rows // row_parts
-    ahead = n_inner // group // 3
+    ahead = 2 * (n_inner // group) // 3
     g_rows, g_sides, g_inner = n_rows // group, n_sides // group, n_inner // group
 
     def row_place(k):
@@ -281,10 +300,17 @@
         return i, j
 
     def node_step(slot, carry):
+        @pl.when(slot == ahead // 2)
+        def _():
+            for index in range(2):
+                received(index, q_copy)
+            each_corner(qbuf, 0, lambda copy: copy.start())
+
         @pl.when(slot == ahead)
         def _():
-            for index in range(len(WAYS)):
+            for index in range(2, 4):
                 received(index, q_copy)
+            each_corner(qbuf, 0, lambda copy: copy.wait_recv())
 
         transform([place(slot, g) for g in range(group)])
 
@@ -293,14 +319,9 @@
             pl.when(exists(WAYS[index]) & (part >= 0) & (part < g_rows))(
                 lambda index=index, part=part: row_copy(index, part).start())
 
-        @pl.when(slot == ahead + g_rows - 1)
-        def _():
-            for index in range(2, 6):
-                where_exists(WAYS[index], lambda index=index: w_copy(index).start())
-
         @pl.when(slot == ahead + g_rows + g_sides - 1)
         def _():
-            for index in range(6, 8):
+            for index in range(2, 4):
                 w_copy(index).start()
 
         return carry
@@ -344,12 +365,19 @@
     for index in range(2):
         for part in range(row_parts):
             received(index, lambda index, part=part: row_copy(index, part))
+    each_corner(wbuf, 1, lambda copy: copy.start())
     for index in range(2, len(WAYS)):
         received(index, w_copy)
 
     def rim_step(t, carry):
+        @pl.when(t == g_sides + row_parts - 2)
+        def _():
+            each_corner(wbuf, 1, lambda copy: copy.wait_recv())
+
+        part = lax.rem(t - g_sides + 1 + row_parts, row_parts)
+        first = jnp.where(t < g_sides, n_rows + t * group, part * group)
         for g in range(group):
-            k = t * group + g
+            k = first + g
             row, side = row_place(jnp.minimum(k, n_rows - 1)), side_place(jnp.maximum(k - n_rows, 0))
             analyse(jnp.where(k < n_rows, row[0], side[0]), jnp.where(k < n_rows, row[1], side[1]))
         return carry
@@ -362,6 +390,8 @@
         else:
             for part in range(row_parts):
                 sent(index, lambda index, part=part: row_copy(index, part))
+    each_corner(qbuf, 0, lambda copy: copy.wait_send())
+    each_corner(wbuf, 1, lambda copy: copy.wait_send())
 
 
 VM = pl.BlockSpec(memory_space=pltpu.VMEM)
@@ -387,12 +417,14 @@
         scratch_shapes=[
             pltpu.VMEM((tile_lat + 2, tile_lon + 2, rows, members), BF16),
             pltpu.VMEM((tile_lat + 2, tile_lon + 2, members, members), BF16),
-            pltpu.SemaphoreType.DMA((8,)),
-            pltpu.SemaphoreType.DMA((8,)),
-            pltpu.SemaphoreType.DMA((8,)),
-            pltpu.SemaphoreType.DMA((8,)),
+            pltpu.SemaphoreType.DMA((4,)),
+            pltpu.SemaphoreType.DMA((4,)),
+            pltpu.SemaphoreType.DMA((4,)),
+            pltpu.SemaphoreType.DMA((4,)),
             pltpu.SemaphoreType.DMA((2, row_parts)),
             pltpu.SemaphoreType.DMA((2, row_parts)),
+            pltpu.SemaphoreType.DMA((2, 4)),
+            pltpu.SemaphoreType.DMA((2, 4)),
         ],
         compiler_params=pltpu.CompilerParams(
             collective_id=0, has_side_effects=True, vmem_limit_bytes=48 * 1024 * 1024

time: 46.1 us -> 44.2 us (0.959)
  Pallas kernels: 44 us -> 42.1 us
    pallas_call x1, Pallas kernels: 40.4 us -> 38.5 us  [body(): pl.pallas_call(functools.partial(main_kernel, counts), out_shape=jax.Shap...]
where the time goes in v2:
time: 44.2 us; the launch traced here: 44 us
  Pallas kernels  42.1 us (95%)
  local copies, waits for them, and re-layouts  1.9 us (4%)
    pallas_call x1, Pallas kernels, body(): pl.pallas_call(functools.partial(main_kernel, counts), out_shape=jax.Shap...  38.5 us
    pallas_call x1, Pallas kernels, body(): pl.pallas_call(prep_kernel, out_shape=jax.ShapeDtypeStruct((tile_lat, til...  3.57 us
    unnamed x13, local copies, waits for them, and re-layouts  1.9 us

profile of v2, /device:TPU:17, one launch (start us, length us, event | category | flops | bytes accessed | tf_op | source)
XLA Modules:
  0.0 44.0 jit_solution(5367094813197793867)
XLA Ops:
  0.0 0.0 copy-start.1
  0.0 0.0 copy-start.5
  0.0 0.0 copy-start.4
  0.0 0.0 copy-start.3
  0.0 0.0 copy-start.2
  0.0 3.6 %prep.1.qx_ref = bf16[4,8,80,128]{3,2,1,0:T(8,128)(2,1)} custom-call(s32[4,8]{1,0:T(4,128)} %count_ref.1, bf16[4,8,64,128]{3,2,1,0:T(8,128)(2,1)} %state_ref.3, s32[4,8,128]{2,1,0:T(8,128)} %row_ref.1, f32[4,8,128]{2,1,0:T(8,128)} %value_ref.1, f32[4,8,128]{2,1,0:T(8,128)} %weight_ref.1), custom_call_target="tpu_custom_call" | custom-call | tf_op jit(solution)/shard_map/prep/pallas_call | solution.py:405
  3.6 0.0 copy-done.1
  3.6 0.0 copy-done.5
  3.6 0.0 copy-done.4
  3.6 0.0 copy-done.3
  3.6 0.0 copy-done.2
  3.6 0.0 copy-start
  3.6 1.1 %copy-done = bf16[4,8,80,128]{3,2,1,0:T(8,128)(2,1)S(1)} copy-done((bf16[4,8,80,128]{3,2,1,0:T(8,128)(2,1)S(1)}, bf16[4,8,80,128]{3,2,1,0:T(8,128)(2,1)}, u32[]{:S(2)}) %copy-start) | copy-done | bytes 655384
  4.7 38.5 %analyse.1 = bf16[4,8,64,128]{3,2,1,0:T(8,128)(2,1)S(1)} custom-call(bf16[4,8,80,128]{3,2,1,0:T(8,128)(2,1)S(1)} %copy-done, bf16[4,8,64,128]{3,2,1,0:T(8,128)(2,1)S(1)} %copy-done.1, s32[4,8,64]{2,1,0:T(8,128)S(1)} %copy-done.2, f32[4,8,64]{2,1,0:T(8,128)S(1)} %copy-done.3, f32[4,8,64]{2,1,0:T(8,128)S(1)} %copy-done.4, s32[4,8,64]{2,1,0:T(8,128)S(1)} %copy-done.5), custom_call_target="tpu_custom_call" | custom-call | tf_op jit(solution)/shard_map/analyse/pallas_call | solution.py:412
  43.2 0.8 %copy.11 = bf16[4,8,64,128]{3,2,1,0:T(8,128)(2,1)} copy(bf16[4,8,64,128]{3,2,1,0:T(8,128)(2,1)S(1)} %analyse.1) | data formatting | bytes 1048576
Async XLA Ops:
  0.0 3.6 %copy-start.1 = (bf16[4,8,64,128]{3,2,1,0:T(8,128)(2,1)S(1)}, bf16[4,8,64,128]{3,2,1,0:T(8,128)(2,1)}, u32[]{:S(2)}) copy-start(bf16[4,8,64,128]{3,2,1,0:T(8,128)(2,1)} %state_ref.3) | copy-start | bytes 1572868
  0.0 3.6 %copy-start.5 = (s32[4,8,64]{2,1,0:T(8,128)S(1)}, s32[4,8,64]{2,1,0:T(8,128)}, u32[]{:S(2)}) copy-start(s32[4,8,64]{2,1,0:T(8,128)} %land_ref.1) | copy-start | bytes 24580
  0.0 3.6 %copy-start.4 = (f32[4,8,64]{2,1,0:T(8,128)S(1)}, f32[4,8,64]{2,1,0:T(8,128)}, u32[]{:S(2)}) copy-start(f32[4,8,64]{2,1,0:T(8,128)} %frac_lon_ref.1) | copy-start | bytes 24580
  0.0 3.6 %copy-start.3 = (f32[4,8,64]{2,1,0:T(8,128)S(1)}, f32[4,8,64]{2,1,0:T(8,128)}, u32[]{:S(2)}) copy-start(f32[4,8,64]{2,1,0:T(8,128)} %frac_lat_ref.1) | copy-start | bytes 24580
  0.0 3.6 %copy-start.2 = (s32[4,8,64]{2,1,0:T(8,128)S(1)}, s32[4,8,64]{2,1,0:T(8,128)}, u32[]{:S(2)}) copy-start(s32[4,8,64]{2,1,0:T(8,128)} %quadrant_ref.1) | copy-start | bytes 24580
  3.6 1.1 %copy-start = (bf16[4,8,80,128]{3,2,1,0:T(8,128)(2,1)S(1)}, bf16[4,8,80,128]{3,2,1,0:T(8,128)(2,1)}, u32[]{:S(2)}) copy-start(bf16[4,8,80,128]{3,2,1,0:T(8,128)(2,1)} %prep.1.qx_ref) | copy-start | bytes 1966084

commit v3 on v2

--- a/solution.py
+++ b/solution.py
@@ -10,7 +10,7 @@
 
 ITERS = 6
 NEAR = (0.5, 1.0, 0.5)
-SIDE_ROWS = 16
+SIDE_ROWS = 8
 F32 = jnp.float32
 BF16 = jnp.bfloat16
 MESH = pl.DeviceIdType.MESH
@@ -38,7 +38,7 @@
     tile_lat, tile_lon, cells, members = state_ref.shape
     slots = row_ref.shape[-1]
     nodes = tile_lat * tile_lon
-    group = group_of(nodes)
+    group = group_of(nodes, 8)
 
     def step(t, carry):
         for g in range(group):
@@ -275,7 +275,7 @@
     mid_lat, mid_lon = tile_lat - 2, tile_lon - 2
     n_rows, n_sides, n_inner = 2 * tile_lon, 2 * mid_lat, mid_lat * mid_lon
     group = n_rows // row_parts
-    ahead = 2 * (n_inner // group) // 3
+    ahead = n_inner // group
     g_rows, g_sides, g_inner = n_rows // group, n_sides // group, n_inner // group
 
     def row_place(k):
@@ -300,7 +300,7 @@
         return i, j
 
     def node_step(slot, carry):
-        @pl.when(slot == ahead // 2)
+        @pl.when(slot == ahead - 1)
         def _():
             for index in range(2):
                 received(index, q_copy)

time: 44.2 us -> 42.5 us (0.962)
  Pallas kernels: 42.1 us -> 40.4 us
    pallas_call x1, Pallas kernels: 38.5 us -> 37.2 us  [body(): pl.pallas_call(functools.partial(main_kernel, counts), out_shape=jax.Shap...]
where the time goes in v3:
time: 42.5 us; the launch traced here: 42.3 us
  Pallas kernels  40.4 us (95%)
  local copies, waits for them, and re-layouts  1.87 us (4%)
    pallas_call x1, Pallas kernels, body(): pl.pallas_call(functools.partial(main_kernel, counts), out_shape=jax.Shap...  37.2 us
    pallas_call x1, Pallas kernels, body(): pl.pallas_call(prep_kernel, out_shape=jax.ShapeDtypeStruct((tile_lat, til...  3.17 us
    unnamed x13, local copies, waits for them, and re-layouts  1.87 us

profile of v3, /device:TPU:17, one launch (start us, length us, event | category | flops | bytes accessed | tf_op | source)
XLA Modules:
  0.0 42.3 jit_solution(11487896579387010698)
XLA Ops:
  0.0 0.0 copy-start.1
  0.0 0.0 copy-start.5
  0.0 0.0 copy-start.4
  0.0 0.0 copy-start.3
  0.0 0.0 copy-start.2
  0.0 3.2 %prep.1.qx_ref = bf16[4,8,72,128]{3,2,1,0:T(8,128)(2,1)} custom-call(s32[4,8]{1,0:T(4,128)} %count_ref.1, bf16[4,8,64,128]{3,2,1,0:T(8,128)(2,1)} %state_ref.3, s32[4,8,128]{2,1,0:T(8,128)} %row_ref.1, f32[4,8,128]{2,1,0:T(8,128)} %value_ref.1, f32[4,8,128]{2,1,0:T(8,128)} %weight_ref.1), custom_call_target="tpu_custom_call" | custom-call | tf_op jit(solution)/shard_map/prep/pallas_call | solution.py:405
  3.2 0.0 copy-done.1
  3.2 0.0 copy-done.5
  3.2 0.0 copy-done.4
  3.2 0.0 copy-done.3
  3.2 0.0 copy-done.2
  3.2 0.0 copy-start
  3.2 1.1 %copy-done = bf16[4,8,72,128]{3,2,1,0:T(8,128)(2,1)S(1)} copy-done((bf16[4,8,72,128]{3,2,1,0:T(8,128)(2,1)S(1)}, bf16[4,8,72,128]{3,2,1,0:T(8,128)(2,1)}, u32[]{:S(2)}) %copy-start) | copy-done | bytes 589848
  4.3 37.2 %analyse.1 = bf16[4,8,64,128]{3,2,1,0:T(8,128)(2,1)S(1)} custom-call(bf16[4,8,72,128]{3,2,1,0:T(8,128)(2,1)S(1)} %copy-done, bf16[4,8,64,128]{3,2,1,0:T(8,128)(2,1)S(1)} %copy-done.1, s32[4,8,64]{2,1,0:T(8,128)S(1)} %copy-done.2, f32[4,8,64]{2,1,0:T(8,128)S(1)} %copy-done.3, f32[4,8,64]{2,1,0:T(8,128)S(1)} %copy-done.4, s32[4,8,64]{2,1,0:T(8,128)S(1)} %copy-done.5), custom_call_target="tpu_custom_call" | custom-call | tf_op jit(solution)/shard_map/analyse/pallas_call | solution.py:412
  41.5 0.8 %copy.11 = bf16[4,8,64,128]{3,2,1,0:T(8,128)(2,1)} copy(bf16[4,8,64,128]{3,2,1,0:T(8,128)(2,1)S(1)} %analyse.1) | data formatting | bytes 1048576
Async XLA Ops:
  0.0 3.2 %copy-start.1 = (bf16[4,8,64,128]{3,2,1,0:T(8,128)(2,1)S(1)}, bf16[4,8,64,128]{3,2,1,0:T(8,128)(2,1)}, u32[]{:S(2)}) copy-start(bf16[4,8,64,128]{3,2,1,0:T(8,128)(2,1)} %state_ref.3) | copy-start | bytes 1572868
  0.0 3.2 %copy-start.5 = (s32[4,8,64]{2,1,0:T(8,128)S(1)}, s32[4,8,64]{2,1,0:T(8,128)}, u32[]{:S(2)}) copy-start(s32[4,8,64]{2,1,0:T(8,128)} %land_ref.1) | copy-start | bytes 24580
  0.0 3.2 %copy-start.4 = (f32[4,8,64]{2,1,0:T(8,128)S(1)}, f32[4,8,64]{2,1,0:T(8,128)}, u32[]{:S(2)}) copy-start(f32[4,8,64]{2,1,0:T(8,128)} %frac_lon_ref.1) | copy-start | bytes 24580
  0.0 3.2 %copy-start.3 = (f32[4,8,64]{2,1,0:T(8,128)S(1)}, f32[4,8,64]{2,1,0:T(8,128)}, u32[]{:S(2)}) copy-start(f32[4,8,64]{2,1,0:T(8,128)} %frac_lat_ref.1) | copy-start | bytes 24580
  0.0 3.2 %copy-start.2 = (s32[4,8,64]{2,1,0:T(8,128)S(1)}, s32[4,8,64]{2,1,0:T(8,128)}, u32[]{:S(2)}) copy-start(s32[4,8,64]{2,1,0:T(8,128)} %quadrant_ref.1) | copy-start | bytes 24580
  3.2 1.1 %copy-start = (bf16[4,8,72,128]{3,2,1,0:T(8,128)(2,1)S(1)}, bf16[4,8,72,128]{3,2,1,0:T(8,128)(2,1)}, u32[]{:S(2)}) copy-start(bf16[4,8,72,128]{3,2,1,0:T(8,128)(2,1)} %prep.1.qx_ref) | copy-start | bytes 1769476
